TPU v7x, 128 devices: a whole 4x4x4 slice. The times are simulated.
128 devices in a mesh: group: 32 (over z, y, x_hi), head: 4 (over x_lo, core).
Axes of the slice: x: 4 (x_hi: 2, x_lo: 2; x = x_hi * 2 + x_lo), y: 4, z: 4, core: 2. Of those that a mesh axis runs over, the one named last changes fastest.
Arguments:
- tokens: bfloat16 [4, 4096, 1536], P(None, 'group'), may hold values from -6 to 6
- parents: int32 [3, 4096], P(None, 'group'), may hold values from 0 to 7
- page_request: int32 [1536], P('group'), may hold values from 0 to 511, as said below
- page_fill: int32 [1536], P('group'), may hold values from 1 to 128, as said below
- keys_pool: bfloat16 [1536, 1536, 128], P('group', 'head'), may hold values from -600 to 600
- values_pool: bfloat16 [1536, 1536, 128], P('group', 'head'), may hold values from -6 to 6
- decay_pool: bfloat16 [1536, 24, 128], P('group', 'head'), may hold values from -494.52 to 0
- gain_attn: float32 [1536], replicated, may hold values from 0.1 to 1.9
- w_query: bfloat16 [1536, 1536], P('head'), may hold values from -0.15625 to 0.15625
- w_key: bfloat16 [1536, 1536], P('head'), may hold values from -0.15625 to 0.15625
- w_value: bfloat16 [1536, 1536], P('head'), may hold values from -0.15625 to 0.15625
- w_forget: bfloat16 [1536, 24], P(None, 'head'), may hold values from -0.15625 to 0.15625
- forget_bias: float32 [24], P('head'), may hold values from -2 to 6
- w_out: bfloat16 [1536, 1536], P('head'), may hold values from -0.15625 to 0.15625
- gain_ffn: float32 [1536], replicated, may hold values from 0.1 to 1.9
- w_gate: bfloat16 [1536, 4096], P(None, 'head'), may hold values from -0.15625 to 0.15625
- w_up: bfloat16 [1536, 4096], P(None, 'head'), may hold values from -0.15625 to 0.15625
- w_down: bfloat16 [4096, 1536], P('head'), may hold values from -0.09375 to 0.09375
Outputs:
- outputs: bfloat16 [4, 4096, 1536], P(None, 'group')
Inputs may be any that keep to these rules, and one draw needn't show every extreme that they name: `page_request`: request ids g * 16 to g * 16 + 15 are the requests owned by group g, and pages g * 48 to g * 48 + 47 are the page slots of group g. The first 32 slots of a group hold pages of its own requests; its other 16 slots hold pages of other groups' requests, at most 1 from the requests of one group. Every request has at least one page. `page_fill`: the valid positions of a page are its first ones.
All inputs are finite; a program needn't handle non-finite values.
Results may differ from a plain program's by a relative error of at most 0.0095.
Values may be sent and summed in bfloat16 or wider, within the bound.
A program may use at most 192 MiB of HBM per device.

v0:
```python
import jax
import jax.numpy as jnp
from jax import lax
from jax.sharding import PartitionSpec as P

BEAMS = 8
OWNED_SLOTS = 32
SPILL = 16
epsilon = 1e-05
masked_score = -1e30


def rms_scale(values, gain_vector):
    widened = values.astype(jnp.float32)
    return (
        widened
        * lax.rsqrt(jnp.mean(widened * widened, axis=-1, keepdims=True) + epsilon)
        * gain_vector
    )


def page_partials(page_keys, page_values, page_decay, fill_count, asked_rows, head_count):
    page_count, inner_width, length = page_keys.shape
    head_size = inner_width // head_count
    keys_split = page_keys.reshape(page_count, head_count, head_size, length)
    values_split = page_values.reshape(page_count, head_count, head_size, length)
    asked_split = asked_rows.reshape(asked_rows.shape[:3] + (head_count, head_size))
    scores = jnp.einsum(
        "pbshd,phdt->pbsht", asked_split, keys_split, preferred_element_type=jnp.float32
    ) * head_size ** (-0.5)
    scores = scores + page_decay.astype(jnp.float32)[:, None, None, :, :]
    valid_mask = jnp.arange(length)[None, :] < fill_count[:, None]
    scores = jnp.where(valid_mask[:, None, None, None, :], scores, masked_score)
    page_top = jnp.max(scores, axis=-1)
    weights = jnp.exp(scores - page_top[..., None])
    page_total = jnp.sum(weights, axis=-1)
    numerator = jnp.einsum(
        "pbsht,phdt->pbshd",
        weights.astype(jnp.bfloat16),
        values_split,
        preferred_element_type=jnp.float32,
    )
    return (page_top, page_total, numerator.reshape(numerator.shape[:3] + (inner_width,)))


def by_request(current_request, page_top, page_total, numerator, request_count, head_count):
    matches = current_request[None, :] == jnp.arange(request_count)[:, None]
    wide_match = matches[:, :, None, None, None]
    best_top = jnp.max(jnp.where(wide_match, page_top[None], masked_score), axis=1)
    factor = jnp.where(wide_match, jnp.exp(page_top[None] - best_top[:, None]), 0.0)
    summed = jnp.sum(factor * page_total[None], axis=1)
    numer_split = numerator.reshape(numerator.shape[:3] + (head_count, -1))
    combined = jnp.sum(factor[..., None] * numer_split[None], axis=1)
    return (best_top, summed, combined.reshape(combined.shape[:3] + (-1,)))


def shards(
    tokens,
    parents,
    page_request,
    page_fill,
    keys_pool,
    values_pool,
    decay_pool,
    gain_attn,
    w_query,
    w_key,
    w_value,
    w_forget,
    forget_bias,
    w_out,
    gain_ffn,
    w_gate,
    w_up,
    w_down,
):
    step_count, row_count, model_width = tokens.shape
    head_count = w_forget.shape[1]
    inner_width = w_query.shape[0]
    head_size = inner_width // head_count
    local_count = row_count // BEAMS
    groups = lax.axis_size("group")
    own_group = lax.axis_index("group")
    capacity = (SPILL + groups - 2) // (groups - 1)
    flat_tokens = tokens.reshape(step_count * row_count, model_width)
    normed = rms_scale(flat_tokens, gain_attn).astype(jnp.bfloat16)

    def project(weight):
        product = lax.dot_general(
            normed, weight, (((1,), (1,)), ((), ())), preferred_element_type=jnp.float32
        )
        return product.astype(jnp.bfloat16).reshape(step_count, row_count, -1)

    queries = project(w_query)
    key_new = project(w_key)
    value_new = project(w_value)
    forget = jax.nn.log_sigmoid(
        jnp.dot(normed, w_forget, preferred_element_type=jnp.float32) + forget_bias
    ).reshape(step_count, row_count, head_count)
    by_row = queries.transpose(1, 0, 2)
    by_request_rows = by_row.reshape(local_count, BEAMS, step_count, inner_width)
    own_request = page_request[:OWNED_SLOTS] - own_group * local_count
    own_parts = page_partials(
        keys_pool[:OWNED_SLOTS],
        values_pool[:OWNED_SLOTS],
        decay_pool[:OWNED_SLOTS],
        page_fill[:OWNED_SLOTS],
        by_request_rows[own_request],
        head_count,
    )
    hosted_request = page_request[OWNED_SLOTS:]
    hosted_owner = hosted_request // local_count
    hosted_local = hosted_request % local_count
    hosted_index = jnp.arange(hosted_request.shape[0])
    earlier = (hosted_owner[:, None] == hosted_owner[None, :]) & (
        hosted_index[None, :] < hosted_index[:, None]
    )
    hosted_rank = jnp.sum(earlier, axis=1)
    slot_match = (hosted_owner[None, None, :] == jnp.arange(groups)[:, None, None]) & (
        hosted_rank[None, None, :] == jnp.arange(capacity)[None, :, None]
    )
    slot_full = jnp.any(slot_match, axis=2)
    slot_source = jnp.sum(jnp.where(slot_match, hosted_index[None, None, :], 0), axis=2)
    slot_local = jnp.sum(jnp.where(slot_match, hosted_local[None, None, :], 0), axis=2)
    slot_count = groups * capacity
    base_rows = jnp.arange(row_count) // BEAMS * BEAMS
    hist_keys = jnp.zeros((0, row_count, inner_width), jnp.bfloat16)
    hist_values = jnp.zeros((0, row_count, inner_width), jnp.bfloat16)
    hist_totals = jnp.zeros((0, row_count, head_count), jnp.float32)
    running = jnp.zeros((row_count, head_count), jnp.float32)
    finished = []
    for step_index in range(step_count):
        query_block = by_row[:, step_index : step_index + 1]
        step_span = query_block.shape[1]
        gathered = lax.all_gather(query_block, "group", axis=0, tiled=True)
        asked_rows = gathered.reshape(groups * local_count, BEAMS, step_span, inner_width)[
            hosted_request
        ]
        page_top, page_total, numerator = page_partials(
            keys_pool[OWNED_SLOTS:],
            values_pool[OWNED_SLOTS:],
            decay_pool[OWNED_SLOTS:],
            page_fill[OWNED_SLOTS:],
            asked_rows,
            head_count,
        )
        full_slot = slot_full[:, :, None, None, None]
        own_now = tuple((member[:, :, step_index : step_index + 1] for member in own_parts))
        all_request = jnp.concatenate(
            [
                own_request,
                lax.all_to_all(
                    slot_local.astype(jnp.float32), "group", split_axis=0, concat_axis=0, tiled=True
                )
                .reshape(slot_count)
                .astype(jnp.int32),
            ],
            axis=0,
        )
        all_top = jnp.concatenate(
            [
                own_now[0],
                lax.all_to_all(
                    jnp.where(full_slot, page_top[slot_source], masked_score),
                    "group",
                    split_axis=0,
                    concat_axis=0,
                    tiled=True,
                ).reshape((slot_count,) + page_top.shape[1:]),
            ],
            axis=0,
        )
        all_total = jnp.concatenate(
            [
                own_now[1],
                lax.all_to_all(
                    jnp.where(full_slot, page_total[slot_source], 0.0),
                    "group",
                    split_axis=0,
                    concat_axis=0,
                    tiled=True,
                ).reshape((slot_count,) + page_total.shape[1:]),
            ],
            axis=0,
        )
        all_numer = jnp.concatenate(
            [
                own_now[2],
                lax.all_to_all(
                    jnp.where(full_slot, numerator[slot_source], 0.0),
                    "group",
                    split_axis=0,
                    concat_axis=0,
                    tiled=True,
                ).reshape((slot_count,) + numerator.shape[1:]),
            ],
            axis=0,
        )
        page_top, page_total, page_numer = by_request(
            all_request, all_top, all_total, all_numer, local_count, head_count
        )
        page_top = page_top.reshape(row_count, head_count)
        page_total = page_total.reshape(row_count, head_count)
        page_numer = page_numer.reshape(row_count, head_count, head_size)
        if step_index > 0:
            source = base_rows + parents[step_index - 1]
            hist_keys = hist_keys[:, source]
            hist_values = hist_values[:, source]
            hist_totals = hist_totals[:, source]
            running = running[source]
        running = running + forget[step_index]
        hist_keys = jnp.concatenate([hist_keys, key_new[step_index][None]], axis=0)
        hist_values = jnp.concatenate([hist_values, value_new[step_index][None]], axis=0)
        hist_totals = jnp.concatenate([hist_totals, running[None]], axis=0)
        asked_now = queries[step_index].reshape(row_count, head_count, head_size)
        keys_now = hist_keys.reshape(step_index + 1, row_count, head_count, head_size)
        values_now = hist_values.reshape(step_index + 1, row_count, head_count, head_size)
        scores = jnp.einsum(
            "rhd,urhd->rhu", asked_now, keys_now, preferred_element_type=jnp.float32
        ) * head_size ** (-0.5) - hist_totals.transpose(1, 2, 0)
        history_top = jnp.max(scores, axis=-1)
        weights = jnp.exp(scores - history_top[..., None])
        history_total = jnp.sum(weights, axis=-1)
        history_numer = jnp.einsum(
            "rhu,urhd->rhd",
            weights.astype(jnp.bfloat16),
            values_now,
            preferred_element_type=jnp.float32,
        )
        best_top = jnp.maximum(page_top, history_top)
        page_scale = jnp.exp(page_top - best_top)
        history_scale = jnp.exp(history_top - best_top)
        total_sum = page_total * page_scale + history_total * history_scale
        numer_sum = page_numer * page_scale[..., None] + history_numer * history_scale[..., None]
        attended = (
            (numer_sum / total_sum[..., None]).astype(jnp.bfloat16).reshape(row_count, inner_width)
        )
        mixed_sum = lax.psum(jnp.dot(attended, w_out, preferred_element_type=jnp.float32), "head")
        residual = tokens[step_index].astype(jnp.float32) + mixed_sum
        normed_ffn = rms_scale(residual, gain_ffn).astype(jnp.bfloat16)
        gate_proj = jnp.dot(normed_ffn, w_gate, preferred_element_type=jnp.float32)
        up_proj = jnp.dot(normed_ffn, w_up, preferred_element_type=jnp.float32)
        hidden = (jax.nn.silu(gate_proj) * up_proj).astype(jnp.bfloat16)
        down_sum = lax.psum(jnp.dot(hidden, w_down, preferred_element_type=jnp.float32), "head")
        finished.append((residual + down_sum).astype(jnp.bfloat16))
    result = jnp.stack(finished, axis=0)
    return result


def solution(mesh):
    return jax.shard_map(
        shards,
        mesh=mesh,
        in_specs=(
            P(None, "group", None),
            P(None, "group"),
            P("group"),
            P("group"),
            P("group", "head", None),
            P("group", "head", None),
            P("group", "head", None),
            P(),
            P("head", None),
            P("head", None),
            P("head", None),
            P(None, "head"),
            P("head"),
            P("head", None),
            P(),
            P(None, "head"),
            P(None, "head"),
            P("head", None),
        ),
        out_specs=P(None, "group", None),
        check_vma=False,
    )
```

profile of v0, /device:TPU:1, one launch (start us, length us, event | category | flops | bytes accessed | tf_op | source)
XLA Modules:
  0.0 839.9 jit_solution(794505036848824269)
XLA Ops:
  19.0 11.5 %all-to-all-start = ((f32[32,1,1]{2,1,0:T(1,128)}), f32[32,1,1]{2,1,0:T(1,128)}, u32[]{:S(2)}, u32[]{:S(2)}) async-start(f32[32,1,1]{2,1,0:T(1,128)} %copy.715), calls=%async_computation | async-start | bytes 32768 | tf_op jit(solution)/shard_map/all_to_all | solution.py:152
  35.8 3.9 slice.193
  43.6 3.7 reshape.1148
  47.3 3.8 bitcast_reduce_fusion
  56.5 4.7 copy.728
  61.2 4.6 reshape.1155
  79.7 2.8 slice.202
  82.5 2.8 slice.198
  140.6 2.8 gather_fusion.23
  179.1 67.7 %all-gather.11.cloned.1.call-done = bf16[4096,1,384]{2,0,1:T(8,128)(2,1)} async-done(((bf16[128,1,384]{2,0,1:T(8,128)(2,1)}), bf16[4096,1,384]{2,0,1:T(8,128)(2,1)}) %all-gather.11.cloned.1.call-update) | async-done | bytes 3145744 | tf_op jit(solution)/shard_map/all_gather | solution.py:135
  254.5 3.3 fusion.162
  259.4 3.4 fusion.164
  270.3 3.3 convolution_bitcast_fusion.2
  277.1 46.8 %all-gather.5.cloned.1.call-done = bf16[4096,1,384]{2,0,1:T(8,128)(2,1)} async-done(((bf16[128,1,384]{2,0,1:T(8,128)(2,1)}), bf16[4096,1,384]{2,0,1:T(8,128)(2,1)}) %all-gather.5.cloned.1.call-update) | async-done | bytes 3145744 | tf_op jit(solution)/shard_map/all_gather | solution.py:135
  372.1 5.6 all-to-all-start.1
  377.7 3.2 convolution_bitcast_fusion.4
  400.3 9.2 %all-to-all-start.4 = ((f32[32,1,8,1,6]{2,3,4,1,0:T(1,128)}), f32[32,1,8,1,6]{2,3,4,1,0:T(1,128)S(1)}, u32[]{:S(2)}, u32[]{:S(2)}) async-start(f32[32,1,8,1,6]{2,3,4,1,0:T(1,128)} %copy.745), calls=%async_computation.4 | async-start | bytes 196608 | tf_op jit(solution)/shard_map/all_to_all | solution.py:163
  409.5 2.7 fusion.69
  418.4 8.4 all-to-all-start.7
  426.9 8.7 %all-to-all-done.7 = f32[32,1,8,1,6]{2,3,4,1,0:T(1,128)S(1)} async-done(((f32[32,1,8,1,6]{2,3,4,1,0:T(1,128)}), f32[32,1,8,1,6]{2,3,4,1,0:T(1,128)S(1)}, u32[]{:S(2)}, u32[]{:S(2)}) %all-to-all-start.7) | async-done | bytes 6176 | tf_op jit(solution)/shard_map/all_to_all | solution.py:163
  435.6 4.3 all-to-all-start.10
  441.5 6.9 all-to-all-done.10
  448.4 3.8 all-to-all-start.3
  453.8 7.3 all-to-all-done.3
  461.1 3.8 all-to-all-start.12
  465.9 8.0 all-to-all-done.12
  473.9 4.5 all-to-all-start.6
  481.4 5.9 all-to-all-done.6
  487.3 4.5 all-to-all-start.9
  503.8 9.2 %all-to-all-start.2 = ((f32[32,1,8,1,384]{4,2,3,1,0:T(8,128)}), f32[32,1,8,1,384]{4,2,3,1,0:T(8,128)S(1)}, u32[]{:S(2)}, u32[]{:S(2)}) async-start(f32[32,1,8,1,384]{4,2,3,1,0:T(8,128)} %get-tuple-element.103), calls=%async_computation.2 | async-start | bytes 786432 | tf_op jit(solution)/shard_map/all_to_all | solution.py:189
  530.5 7.8 exponential_select_fusion.1
  539.5 9.3 %all-to-all-start.5 = ((f32[32,1,8,1,384]{4,2,3,1,0:T(8,128)}), f32[32,1,8,1,384]{4,2,3,1,0:T(8,128)}, u32[]{:S(2)}, u32[]{:S(2)}) async-start(f32[32,1,8,1,384]{4,2,3,1,0:T(8,128)} %get-tuple-element.101), calls=%async_computation.5 | async-start | bytes 786432 | tf_op jit(solution)/shard_map/all_to_all | solution.py:189
  552.9 7.7 multiply_reduce_fusion.3
  561.9 9.2 %all-to-all-start.11 = ((f32[32,1,8,1,384]{4,2,3,1,0:T(8,128)}), f32[32,1,8,1,384]{4,2,3,1,0:T(8,128)S(1)}, u32[]{:S(2)}, u32[]{:S(2)}) async-start(f32[32,1,8,1,384]{4,2,3,1,0:T(8,128)} %get-tuple-element.102), calls=%async_computation.11 | async-start | bytes 786432 | tf_op jit(solution)/shard_map/all_to_all | solution.py:189
  577.7 7.7 multiply_reduce_fusion.2
  590.9 9.3 %all-to-all-start.8 = ((f32[32,1,8,1,384]{4,2,3,1,0:T(8,128)}), f32[32,1,8,1,384]{4,2,3,1,0:T(8,128)}, u32[]{:S(2)}, u32[]{:S(2)}) async-start(f32[32,1,8,1,384]{4,2,3,1,0:T(8,128)} %get-tuple-element.100), calls=%async_computation.8 | async-start | bytes 786432 | tf_op jit(solution)/shard_map/all_to_all | solution.py:189
  604.5 7.7 multiply_reduce_fusion
  620.3 7.7 multiply_reduce_fusion.1
  631.2 88.7 %all-reduce.7.cloned.1.call-done = (f32[128,1536]{1,0:T(8,128)}, f32[128,1536]{1,0:T(8,128)}, f32[128,1536]{1,0:T(8,128)}, f32[128,1536]{1,0:T(8,128)}) async-done(((f32[128,1536]{1,0:T(8,128)}, f32[128,1536]{1,0:T(8,128)}, f32[128,1536]{1,0:T(8,128)}, f32[128,1536]{1,0:T(8,128)}), (f32[128,1536]{1,0:T(8,128)}, f32[128,1536]{1,0:T(8,128)}, f32[128,1536]{1,0:T(8,128)}, ...) | async-done | bytes 3145744 | tf_op jit(solution)/shard_map/psum | solution.py:238
  719.9 3.0 multiply_reduce_fusion.10
  728.4 4.1 fusion.33
  732.5 4.1 fusion.34
  736.5 3.4 fusion.169
  739.9 4.1 fusion.35
  744.1 3.3 fusion.167
  747.3 4.0 fusion.36
  751.3 76.1 %all-reduce.5.cloned.1.call-done = (f32[128,1536]{1,0:T(8,128)}, f32[128,1536]{1,0:T(8,128)}, f32[128,1536]{1,0:T(8,128)}, f32[128,1536]{1,0:T(8,128)}) async-done(((f32[128,1536]{1,0:T(8,128)}, f32[128,1536]{1,0:T(8,128)}, f32[128,1536]{1,0:T(8,128)}, f32[128,1536]{1,0:T(8,128)}), (f32[128,1536]{1,0:T(8,128)}, f32[128,1536]{1,0:T(8,128)}, f32[128,1536]{1,0:T(8,128)}, ...) | async-done | bytes 3145744 | tf_op jit(solution)/shard_map/psum | solution.py:244
  827.4 4.1 fusion.58
  (463 shorter events, 302.6 us)
Async XLA Ops:
  6.5 721.9 %copy-start = (bf16[1024,1536]{1,0:T(8,128)(2,1)S(1)}, bf16[1024,1536]{1,0:T(8,128)(2,1)}, u32[]{:S(2)}) copy-start(bf16[1024,1536]{1,0:T(8,128)(2,1)} %param.35) | copy-start | bytes 9437188
  6.5 165.9 %all-gather.9.cloned.1.call-start = ((), (), s32[]{:S(2)}) async-start(), calls=%async_computation.15 | async-start | bytes 3244032 | tf_op jit(solution)/shard_map/all_gather | solution.py:135
  15.1 160.7 %all-gather.7.cloned.1.call-start = ((), (), s32[]{:S(2)}) async-start(), calls=%async_computation.14 | async-start | bytes 3244032 | tf_op jit(solution)/shard_map/all_gather | solution.py:135
  15.8 231.1 %all-gather.11.cloned.1.call-start = ((), (), s32[]{:S(2)}) async-start(), calls=%async_computation.16 | async-start | bytes 3244032 | tf_op jit(solution)/shard_map/all_gather | solution.py:135
  17.6 17.3 %copy-start.87 = (pred[16]{0:T(512)(128)(4,1)}, pred[16]{0:T(512)(128)(4,1)S(1)}, u32[]{:S(2)}) copy-start(pred[16]{0:T(512)(128)(4,1)S(1)} %broadcast_compare_fusion) | copy-start | bytes 52
  19.0 150.7 %all-to-all-start = ((f32[32,1,1]{2,1,0:T(1,128)}), f32[32,1,1]{2,1,0:T(1,128)}, u32[]{:S(2)}, u32[]{:S(2)}) async-start(f32[32,1,1]{2,1,0:T(1,128)} %copy.715), calls=%async_computation | async-start | bytes 32768 | tf_op jit(solution)/shard_map/all_to_all | solution.py:152
  30.4 293.4 %all-gather.5.cloned.1.call-start = ((), (), s32[]{:S(2)}) async-start(), calls=%async_computation.13 | async-start | bytes 3244032 | tf_op jit(solution)/shard_map/all_gather | solution.py:135
  87.7 21.9 %copy-start.39 = (f32[32,8,1,6]{1,2,3,0:T(1,128)S(1)}, f32[32,8,1,6]{1,2,3,0:T(1,128)}, u32[]{:S(2)}) copy-start(f32[32,8,1,6]{1,2,3,0:T(1,128)} %get-tuple-element.76) | copy-start | bytes 18436
  105.5 19.6 %copy-start.69 = (f32[128,6]{0,1:T(8,128)S(1)}, f32[128,6]{0,1:T(8,128)}, u32[]{:S(2)}) copy-start(f32[128,6]{0,1:T(8,128)} %copy.815) | copy-start | bytes 9220
  106.5 20.0 %copy-start.53 = (f32[128,6]{0,1:T(8,128)S(1)}, f32[128,6]{0,1:T(8,128)}, u32[]{:S(2)}) copy-start(f32[128,6]{0,1:T(8,128)} %slice_add_fusion.1) | copy-start | bytes 9220
  140.6 14.2 %copy-start.33 = (bf16[2,128,384]{1,2,0:T(8,128)(2,1)S(1)}, bf16[2,128,384]{1,2,0:T(8,128)(2,1)}, u32[]{:S(2)}) copy-start(bf16[2,128,384]{1,2,0:T(8,128)(2,1)} %copy.782) | copy-start | bytes 589828
  148.1 18.0 %copy-start.79 = (s32[16]{0:T(128)S(1)}, s32[16]{0:T(128)}, u32[]{:S(2)}) copy-start(s32[16]{0:T(128)} %copy-done.78) | copy-start | bytes 196
  166.1 226.7 %copy-start.56 = (s32[1024]{0:T(1024)}, s32[1024]{0:T(1024)S(1)}, u32[]{:S(2)}) copy-start(s32[1024]{0:T(1024)S(1)} %pad_clamp_fusion.3) | copy-start | bytes 12292
  264.4 10.9 %copy-start.30 = (f32[16,8,6]{1,2,0:T(8,128)S(1)}, f32[16,8,6]{1,2,0:T(8,128)}, u32[]{:S(2)}) copy-start(f32[16,8,6]{1,2,0:T(8,128)} %get-tuple-element.119) | copy-start | bytes 9220
  327.2 41.9 %copy-start.81 = (pred[32]{0:T(512)(128)(4,1)S(1)}, pred[32]{0:T(512)(128)(4,1)}, u32[]{:S(2)}) copy-start(pred[32]{0:T(512)(128)(4,1)} %fusion.115) | copy-start | bytes 100
  372.1 28.2 %all-to-all-start.1 = ((f32[32,1,8,1,6]{2,3,4,1,0:T(1,128)}), f32[32,1,8,1,6]{2,3,4,1,0:T(1,128)}, u32[]{:S(2)}, u32[]{:S(2)}) async-start(f32[32,1,8,1,6]{2,3,4,1,0:T(1,128)} %copy.724), calls=%async_computation.1 | async-start | bytes 196608 | tf_op jit(solution)/shard_map/all_to_all | solution.py:163
  388.3 21.1 %copy-start.82 = (pred[32]{0:T(512)(128)(4,1)S(1)}, pred[32]{0:T(512)(128)(4,1)}, u32[]{:S(2)}) copy-start(pred[32]{0:T(512)(128)(4,1)} %fusion.115) | copy-start | bytes 100
  394.1 19.5 %copy-start.49 = (f32[32,1,8,1,6]{0,2,4,3,1:T(8,128)S(1)}, f32[32,1,8,1,6]{0,2,4,3,1:T(8,128)}, u32[]{:S(2)}) copy-start(f32[32,1,8,1,6]{0,2,4,3,1:T(8,128)} %get-tuple-element.110) | copy-start | bytes 18436
  394.1 20.3 %copy-start.48 = (f32[32,1,8,1,6]{0,2,4,3,1:T(8,128)S(1)}, f32[32,1,8,1,6]{0,2,4,3,1:T(8,128)}, u32[]{:S(2)}) copy-start(f32[32,1,8,1,6]{0,2,4,3,1:T(8,128)} %get-tuple-element.107) | copy-start | bytes 18436
  394.1 21.0 %copy-start.47 = (f32[32,1,8,1,6]{0,2,4,3,1:T(8,128)S(1)}, f32[32,1,8,1,6]{0,2,4,3,1:T(8,128)}, u32[]{:S(2)}) copy-start(f32[32,1,8,1,6]{0,2,4,3,1:T(8,128)} %get-tuple-element.109) | copy-start | bytes 18436
  394.1 21.7 %copy-start.46 = (f32[32,1,8,1,6]{0,2,4,3,1:T(8,128)S(1)}, f32[32,1,8,1,6]{0,2,4,3,1:T(8,128)}, u32[]{:S(2)}) copy-start(f32[32,1,8,1,6]{0,2,4,3,1:T(8,128)} %get-tuple-element.104) | copy-start | bytes 18436
  396.0 30.8 %copy-start.44 = (f32[32,8,1,6]{0,1,3,2:T(8,128)S(1)}, f32[32,8,1,6]{0,1,3,2:T(8,128)}, u32[]{:S(2)}) copy-start(f32[32,8,1,6]{0,1,3,2:T(8,128)} %copy.726) | copy-start | bytes 18436
  396.0 30.8 %copy-start.45 = (f32[32,8,1,6]{0,1,3,2:T(8,128)S(1)}, f32[32,8,1,6]{0,1,3,2:T(8,128)}, u32[]{:S(2)}) copy-start(f32[32,8,1,6]{0,1,3,2:T(8,128)} %copy.747) | copy-start | bytes 18436
  397.2 55.7 %copy-start.42 = (f32[32,8,1,6]{0,1,3,2:T(8,128)S(1)}, f32[32,8,1,6]{0,1,3,2:T(8,128)}, u32[]{:S(2)}) copy-start(f32[32,8,1,6]{0,1,3,2:T(8,128)} %copy.773) | copy-start | bytes 18436
  397.2 55.7 %copy-start.43 = (f32[32,8,1,6]{0,1,3,2:T(8,128)S(1)}, f32[32,8,1,6]{0,1,3,2:T(8,128)}, u32[]{:S(2)}) copy-start(f32[32,8,1,6]{0,1,3,2:T(8,128)} %copy.805) | copy-start | bytes 18436
  398.8 13.4 %copy-start.51 = (f32[32,1,8,1,6]{0,2,4,3,1:T(8,128)S(1)}, f32[32,1,8,1,6]{0,2,4,3,1:T(8,128)}, u32[]{:S(2)}) copy-start(f32[32,1,8,1,6]{0,2,4,3,1:T(8,128)} %get-tuple-element.105) | copy-start | bytes 18436
  398.8 14.1 %copy-start.50 = (f32[32,1,8,1,6]{0,2,4,3,1:T(8,128)S(1)}, f32[32,1,8,1,6]{0,2,4,3,1:T(8,128)}, u32[]{:S(2)}) copy-start(f32[32,1,8,1,6]{0,2,4,3,1:T(8,128)} %get-tuple-element.108) | copy-start | bytes 18436
  400.3 18.1 %all-to-all-start.4 = ((f32[32,1,8,1,6]{2,3,4,1,0:T(1,128)}), f32[32,1,8,1,6]{2,3,4,1,0:T(1,128)S(1)}, u32[]{:S(2)}, u32[]{:S(2)}) async-start(f32[32,1,8,1,6]{2,3,4,1,0:T(1,128)} %copy.745), calls=%async_computation.4 | async-start | bytes 196608 | tf_op jit(solution)/shard_map/all_to_all | solution.py:163
  418.4 17.3 %all-to-all-start.7 = ((f32[32,1,8,1,6]{2,3,4,1,0:T(1,128)}), f32[32,1,8,1,6]{2,3,4,1,0:T(1,128)S(1)}, u32[]{:S(2)}, u32[]{:S(2)}) async-start(f32[32,1,8,1,6]{2,3,4,1,0:T(1,128)} %copy.771), calls=%async_computation.7 | async-start | bytes 196608 | tf_op jit(solution)/shard_map/all_to_all | solution.py:163
  426.9 76.8 %copy-start.34 = (f32[64,8,6]{0,1,2:T(8,128)}, f32[64,8,6]{0,1,2:T(8,128)S(1)}, u32[]{:S(2)}) copy-start(f32[64,8,6]{0,1,2:T(8,128)S(1)} %get-tuple-element.124) | copy-start | bytes 36868
  435.6 12.7 %all-to-all-start.10 = ((f32[32,1,8,1,6]{2,3,4,1,0:T(1,128)}), f32[32,1,8,1,6]{2,3,4,1,0:T(1,128)S(1)}, u32[]{:S(2)}, u32[]{:S(2)}) async-start(f32[32,1,8,1,6]{2,3,4,1,0:T(1,128)} %copy.803), calls=%async_computation.10 | async-start | bytes 196608 | tf_op jit(solution)/shard_map/all_to_all | solution.py:163
  440.8 62.9 %copy-start.27 = (f32[16,8,6]{1,2,0:T(8,128)}, f32[16,8,6]{1,2,0:T(8,128)S(1)}, u32[]{:S(2)}) copy-start(f32[16,8,6]{1,2,0:T(8,128)S(1)} %select_reduce_fusion.3) | copy-start | bytes 9220
  448.4 12.7 %all-to-all-start.3 = ((f32[32,1,8,1,6]{2,3,4,1,0:T(1,128)}), f32[32,1,8,1,6]{2,3,4,1,0:T(1,128)S(1)}, u32[]{:S(2)}, u32[]{:S(2)}) async-start(f32[32,1,8,1,6]{2,3,4,1,0:T(1,128)} %copy.737), calls=%async_computation.3 | async-start | bytes 196608 | tf_op jit(solution)/shard_map/all_to_all | solution.py:176
  453.7 50.0 %copy-start.35 = (f32[64,8,6]{0,1,2:T(8,128)}, f32[64,8,6]{0,1,2:T(8,128)S(1)}, u32[]{:S(2)}) copy-start(f32[64,8,6]{0,1,2:T(8,128)S(1)} %get-tuple-element.125) | copy-start | bytes 36868
  453.8 50.0 %copy-start.36 = (f32[64,8,6]{0,1,2:T(8,128)}, f32[64,8,6]{0,1,2:T(8,128)S(1)}, u32[]{:S(2)}) copy-start(f32[64,8,6]{0,1,2:T(8,128)S(1)} %get-tuple-element.126) | copy-start | bytes 36868
  461.1 12.8 %all-to-all-start.12 = ((f32[32,1,8,1,6]{2,3,4,1,0:T(1,128)}), f32[32,1,8,1,6]{2,3,4,1,0:T(1,128)S(1)}, u32[]{:S(2)}, u32[]{:S(2)}) async-start(f32[32,1,8,1,6]{2,3,4,1,0:T(1,128)} %copy.826), calls=%async_computation.12 | async-start | bytes 196608 | tf_op jit(solution)/shard_map/all_to_all | solution.py:176
  473.9 13.4 %all-to-all-start.6 = ((f32[32,1,8,1,6]{2,3,4,1,0:T(1,128)}), f32[32,1,8,1,6]{2,3,4,1,0:T(1,128)}, u32[]{:S(2)}, u32[]{:S(2)}) async-start(f32[32,1,8,1,6]{2,3,4,1,0:T(1,128)} %copy.763), calls=%async_computation.6 | async-start | bytes 196608 | tf_op jit(solution)/shard_map/all_to_all | solution.py:176
  480.4 23.4 %copy-start.24 = (f32[16,8,6]{1,2,0:T(8,128)}, f32[16,8,6]{1,2,0:T(8,128)S(1)}, u32[]{:S(2)}) copy-start(f32[16,8,6]{1,2,0:T(8,128)S(1)} %get-tuple-element.10) | copy-start | bytes 9220
  480.4 23.4 %copy-start.25 = (f32[16,8,6]{1,2,0:T(8,128)}, f32[16,8,6]{1,2,0:T(8,128)S(1)}, u32[]{:S(2)}) copy-start(f32[16,8,6]{1,2,0:T(8,128)S(1)} %get-tuple-element.11) | copy-start | bytes 9220
  480.4 23.4 %copy-start.26 = (f32[16,8,6]{1,2,0:T(8,128)}, f32[16,8,6]{1,2,0:T(8,128)S(1)}, u32[]{:S(2)}) copy-start(f32[16,8,6]{1,2,0:T(8,128)S(1)} %get-tuple-element.12) | copy-start | bytes 9220
  487.3 16.4 %all-to-all-start.9 = ((f32[32,1,8,1,6]{2,3,4,1,0:T(1,128)}), f32[32,1,8,1,6]{2,3,4,1,0:T(1,128)}, u32[]{:S(2)}, u32[]{:S(2)}) async-start(f32[32,1,8,1,6]{2,3,4,1,0:T(1,128)} %copy.794), calls=%async_computation.9 | async-start | bytes 196608 | tf_op jit(solution)/shard_map/all_to_all | solution.py:176
  503.8 35.7 %all-to-all-start.2 = ((f32[32,1,8,1,384]{4,2,3,1,0:T(8,128)}), f32[32,1,8,1,384]{4,2,3,1,0:T(8,128)S(1)}, u32[]{:S(2)}, u32[]{:S(2)}) async-start(f32[32,1,8,1,384]{4,2,3,1,0:T(8,128)} %get-tuple-element.103), calls=%async_computation.2 | async-start | bytes 786432 | tf_op jit(solution)/shard_map/all_to_all | solution.py:189
  539.5 22.4 %all-to-all-start.5 = ((f32[32,1,8,1,384]{4,2,3,1,0:T(8,128)}), f32[32,1,8,1,384]{4,2,3,1,0:T(8,128)}, u32[]{:S(2)}, u32[]{:S(2)}) async-start(f32[32,1,8,1,384]{4,2,3,1,0:T(8,128)} %get-tuple-element.101), calls=%async_computation.5 | async-start | bytes 786432 | tf_op jit(solution)/shard_map/all_to_all | solution.py:189
  561.9 28.9 %all-to-all-start.11 = ((f32[32,1,8,1,384]{4,2,3,1,0:T(8,128)}), f32[32,1,8,1,384]{4,2,3,1,0:T(8,128)S(1)}, u32[]{:S(2)}, u32[]{:S(2)}) async-start(f32[32,1,8,1,384]{4,2,3,1,0:T(8,128)} %get-tuple-element.102), calls=%async_computation.11 | async-start | bytes 786432 | tf_op jit(solution)/shard_map/all_to_all | solution.py:189
  590.9 24.4 %all-to-all-start.8 = ((f32[32,1,8,1,384]{4,2,3,1,0:T(8,128)}), f32[32,1,8,1,384]{4,2,3,1,0:T(8,128)}, u32[]{:S(2)}, u32[]{:S(2)}) async-start(f32[32,1,8,1,384]{4,2,3,1,0:T(8,128)} %get-tuple-element.100), calls=%async_computation.8 | async-start | bytes 786432 | tf_op jit(solution)/shard_map/all_to_all | solution.py:189
  600.2 119.6 %all-reduce.7.cloned.1.call-start = ((), (), s32[]{:S(2)}) async-start(), calls=%async_computation.18 | async-start | bytes 6291456 | tf_op jit(solution)/shard_map/psum | solution.py:238
  631.1 91.7 %copy-start.76 = (f32[1536]{0:T(1024)S(1)}, f32[1536]{0:T(1024)}, u32[]{:S(2)}) copy-start(f32[1536]{0:T(1024)} %param.32) | copy-start | bytes 18436
  631.1 196.3 %all-reduce.5.cloned.1.call-start = ((), (), s32[]{:S(2)}) async-start(), calls=%async_computation.17 | async-start | bytes 6291456 | tf_op jit(solution)/shard_map/psum | solution.py:244
  (63 other events, 326.7 us)
Sparse Core Ops, SparseCore 0:
  15.2 77.4 all-gather.8
  95.7 74.0 all-gather.6
  172.8 74.0 all-gather.10
  249.7 74.0 all-gather.4
  631.3 88.5 all-reduce.6
  751.5 75.9 all-reduce.4
where the time goes:
time: 854 us; the launch traced here: 840 us
  waiting for transfers between devices  319 us (37%)
  local copies, waits for them, and re-layouts  223 us (26%)
  other arithmetic  123 us (14%)
  starting transfers between devices  93.1 us (11%)
  matrix products  66.5 us (8%)
  between operations  14.9 us (2%)
    all_gather x4, waiting for transfers between devices, shards(): gathered = lax.all_gather(query_block, 'group', axis=0, tiled=True)  115 us
    psum x1, waiting for transfers between devices, shards(): lax.psum(jnp.dot(attended, w_out, preferred_element_type=jnp.float32), 'h...  88.7 us
    psum x1, waiting for transfers between devices, shards(): lax.psum(jnp.dot(hidden, w_down, preferred_element_type=jnp.float32), 'he...  76.1 us
    all_to_all x4, starting transfers between devices, shards(): lax.all_to_all(jnp.where(full_slot, numerator[slot_source], 0.0), 'group'...  37 us
    reduce_sum x4, other arithmetic, by_request(): combined = jnp.sum(factor[..., None] * numer_split[None], axis=1)  30.9 us
    all_to_all x4, starting transfers between devices, shards(): lax.all_to_all(jnp.where(full_slot, page_top[slot_source], masked_score),...  27.4 us
    all_to_all x4, waiting for transfers between devices, shards(): lax.all_to_all(jnp.where(full_slot, page_total[slot_source], 0.0), 'group...  21.2 us
  transfers between devices with their start and end apart: 19, of which 11 were waited for; matrix products, arithmetic and copies ran while one was open for 36% of the time, Pallas kernels for 0%

commit v1 on v0

--- a/solution.py
+++ b/solution.py
@@ -132,7 +132,8 @@
     for step_index in range(step_count):
         query_block = by_row[:, step_index : step_index + 1]
         step_span = query_block.shape[1]
-        gathered = lax.all_gather(query_block, "group", axis=0, tiled=True)
+        sent = jnp.stack([query_block] * lax.axis_size("group"))
+        gathered = jnp.concatenate(lax.all_to_all(sent, "group", 0, 0), axis=0)
         asked_rows = gathered.reshape(groups * local_count, BEAMS, step_span, inner_width)[
             hosted_request
         ]

time: 854 us -> 813 us (0.952)
  waiting for transfers between devices: 319 us -> 225 us
  starting transfers between devices: 93.1 us -> 129 us
  local copies, waits for them, and re-layouts: 223 us -> 239 us
    all_gather x4 -> x0, waiting for transfers between devices: 115 us -> none  [shards(): gathered = lax.all_gather(query_block, 'group', axis=0, tiled=True)]
    all_to_all x0 -> x4, starting transfers between devices: none -> 33.7 us  [shards(): gathered = jnp.concatenate(lax.all_to_all(sent, 'group', 0, 0), axis=0)]
    all_to_all x0 -> x4, waiting for transfers between devices: none -> 23.5 us  [shards(): gathered = jnp.concatenate(lax.all_to_all(sent, 'group', 0, 0), axis=0)]
    another operation x4 -> x8, local copies, waits for them, and re-layouts: 3.51 us -> 14.9 us  [the longest x4 11.4 us: shards(): sent = jnp.stack([query_block] * lax.axis_size('group'))]
  transfers between devices with their start and end apart: 19 -> 19, of which waited for: 11 -> 11; matrix products, arithmetic and copies ran while one was open for 36% -> 39% of each run, Pallas kernels for 0% -> 0%
where the time goes in v1:
time: 813 us; the launch traced here: 801 us
  local copies, waits for them, and re-layouts  239 us (29%)
  waiting for transfers between devices  225 us (28%)
  starting transfers between devices  129 us (16%)
  other arithmetic  119 us (15%)
  matrix products  72.7 us (9%)
  between operations  14.9 us (2%)
    psum x1, waiting for transfers between devices, shards(): lax.psum(jnp.dot(attended, w_out, preferred_element_type=jnp.float32), 'h...  87.6 us
    psum x1, waiting for transfers between devices, shards(): lax.psum(jnp.dot(hidden, w_down, preferred_element_type=jnp.float32), 'he...  76.1 us
    all_to_all x4, starting transfers between devices, shards(): lax.all_to_all(jnp.where(full_slot, numerator[slot_source], 0.0), 'group'...  37 us
    all_to_all x4, starting transfers between devices, shards(): gathered = jnp.concatenate(lax.all_to_all(sent, 'group', 0, 0), axis=0)  33.7 us
    reduce_sum x4, other arithmetic, by_request(): combined = jnp.sum(factor[..., None] * numer_split[None], axis=1)  30.9 us
    all_to_all x4, starting transfers between devices, shards(): lax.all_to_all(jnp.where(full_slot, page_top[slot_source], masked_score),...  30.1 us
    all_to_all x4, waiting for transfers between devices, shards(): gathered = jnp.concatenate(lax.all_to_all(sent, 'group', 0, 0), axis=0)  23.5 us
    all_to_all x4, waiting for transfers between devices, shards(): lax.all_to_all(jnp.where(full_slot, page_total[slot_source], 0.0), 'group...  21.3 us
  transfers between devices with their start and end apart: 19, of which 11 were waited for; matrix products, arithmetic and copies ran while one was open for 39% of the time, Pallas kernels for 0%

profile of v1, /device:TPU:1, one launch (start us, length us, event | category | flops | bytes accessed | tf_op | source)
XLA Modules:
  0.0 800.7 jit_solution(6131655672038056932)
XLA Ops:
  9.8 11.3 %all-to-all-start = ((f32[32,1,1]{2,1,0:T(1,128)}), f32[32,1,1]{2,1,0:T(1,128)S(1)}, u32[]{:S(2)}, u32[]{:S(2)}) async-start(f32[32,1,1]{2,1,0:T(1,128)} %copy.719), calls=%async_computation | async-start | bytes 32768 | tf_op jit(solution)/shard_map/all_to_all | solution.py:153
  32.6 9.3 %all-to-all-start.9 = ((bf16[32,128,1,384]{3,1,2,0:T(8,128)(2,1)}), bf16[32,128,1,384]{3,1,2,0:T(8,128)(2,1)}, u32[]{:S(2)}, u32[]{:S(2)}) async-start(bf16[32,128,1,384]{3,1,2,0:T(8,128)(2,1)} %stack.22), calls=%async_computation.9 | async-start | bytes 6291456 | tf_op jit(solution)/shard_map/all_to_all | solution.py:136
  43.6 4.0 slice.201
  51.5 3.8 reshape.1148
  58.2 3.8 bitcast_reduce_fusion
  63.8 3.5 convolution_bitcast_fusion
  67.2 14.7 %all-to-all-done.9 = bf16[32,128,1,384]{3,1,2,0:T(8,128)(2,1)} async-done(((bf16[32,128,1,384]{3,1,2,0:T(8,128)(2,1)}), bf16[32,128,1,384]{3,1,2,0:T(8,128)(2,1)}, u32[]{:S(2)}, u32[]{:S(2)}) %all-to-all-start.9) | async-done | bytes 3145760 | tf_op jit(solution)/shard_map/all_to_all | solution.py:136
  84.2 7.4 all-to-all-start.5
  92.2 6.6 copy.732
  98.8 4.5 reshape.1154
  123.9 7.5 all-to-all-done.5
  134.6 7.3 all-to-all-start.13
  232.9 9.7 %all-to-all-start.1 = ((bf16[32,128,1,384]{3,1,2,0:T(8,128)(2,1)}), bf16[32,128,1,384]{3,1,2,0:T(8,128)(2,1)}, u32[]{:S(2)}, u32[]{:S(2)}) async-start(bf16[32,128,1,384]{3,1,2,0:T(8,128)(2,1)} %stack.18), calls=%async_computation.1 | async-start | bytes 6291456 | tf_op jit(solution)/shard_map/all_to_all | solution.py:136
  258.4 3.3 fusion.161
  263.3 3.3 fusion.163
  274.2 3.3 convolution_bitcast_fusion.2
  330.6 8.2 %all-to-all-start.2 = ((f32[32,1,8,1,6]{2,3,4,1,0:T(1,128)}), f32[32,1,8,1,6]{2,3,4,1,0:T(1,128)}, u32[]{:S(2)}, u32[]{:S(2)}) async-start(f32[32,1,8,1,6]{2,3,4,1,0:T(1,128)} %copy.728), calls=%async_computation.2 | async-start | bytes 196608 | tf_op jit(solution)/shard_map/all_to_all | solution.py:164
  338.9 3.2 convolution_bitcast_fusion.4
  361.5 9.2 %all-to-all-start.6 = ((f32[32,1,8,1,6]{2,3,4,1,0:T(1,128)}), f32[32,1,8,1,6]{2,3,4,1,0:T(1,128)S(1)}, u32[]{:S(2)}, u32[]{:S(2)}) async-start(f32[32,1,8,1,6]{2,3,4,1,0:T(1,128)} %copy.749), calls=%async_computation.6 | async-start | bytes 196608 | tf_op jit(solution)/shard_map/all_to_all | solution.py:164
  379.6 8.4 %all-to-all-start.10 = ((f32[32,1,8,1,6]{2,3,4,1,0:T(1,128)}), f32[32,1,8,1,6]{2,3,4,1,0:T(1,128)S(1)}, u32[]{:S(2)}, u32[]{:S(2)}) async-start(f32[32,1,8,1,6]{2,3,4,1,0:T(1,128)} %copy.775), calls=%async_computation.10 | async-start | bytes 196608 | tf_op jit(solution)/shard_map/all_to_all | solution.py:164
  388.2 8.7 %all-to-all-done.10 = f32[32,1,8,1,6]{2,3,4,1,0:T(1,128)S(1)} async-done(((f32[32,1,8,1,6]{2,3,4,1,0:T(1,128)}), f32[32,1,8,1,6]{2,3,4,1,0:T(1,128)S(1)}, u32[]{:S(2)}, u32[]{:S(2)}) %all-to-all-start.10) | async-done | bytes 6176 | tf_op jit(solution)/shard_map/all_to_all | solution.py:164
  396.9 4.3 all-to-all-start.14
  402.7 7.4 all-to-all-done.14
  410.1 3.8 all-to-all-start.4
  415.5 7.3 all-to-all-done.4
  422.9 3.8 all-to-all-start.16
  427.6 8.0 all-to-all-done.16
  435.6 4.6 all-to-all-start.8
  443.1 5.9 all-to-all-done.8
  449.1 4.6 all-to-all-start.12
  465.6 9.2 %all-to-all-start.3 = ((f32[32,1,8,1,384]{4,2,3,1,0:T(8,128)}), f32[32,1,8,1,384]{4,2,3,1,0:T(8,128)S(1)}, u32[]{:S(2)}, u32[]{:S(2)}) async-start(f32[32,1,8,1,384]{4,2,3,1,0:T(8,128)} %get-tuple-element.103), calls=%async_computation.3 | async-start | bytes 786432 | tf_op jit(solution)/shard_map/all_to_all | solution.py:190
  492.3 7.8 exponential_select_fusion.1
  501.4 9.3 %all-to-all-start.7 = ((f32[32,1,8,1,384]{4,2,3,1,0:T(8,128)}), f32[32,1,8,1,384]{4,2,3,1,0:T(8,128)}, u32[]{:S(2)}, u32[]{:S(2)}) async-start(f32[32,1,8,1,384]{4,2,3,1,0:T(8,128)} %get-tuple-element.101), calls=%async_computation.7 | async-start | bytes 786432 | tf_op jit(solution)/shard_map/all_to_all | solution.py:190
  514.7 7.7 multiply_reduce_fusion.3
  523.8 9.2 %all-to-all-start.15 = ((f32[32,1,8,1,384]{4,2,3,1,0:T(8,128)}), f32[32,1,8,1,384]{4,2,3,1,0:T(8,128)S(1)}, u32[]{:S(2)}, u32[]{:S(2)}) async-start(f32[32,1,8,1,384]{4,2,3,1,0:T(8,128)} %get-tuple-element.102), calls=%async_computation.15 | async-start | bytes 786432 | tf_op jit(solution)/shard_map/all_to_all | solution.py:190
  539.6 7.7 multiply_reduce_fusion.2
  552.7 9.3 %all-to-all-start.11 = ((f32[32,1,8,1,384]{4,2,3,1,0:T(8,128)}), f32[32,1,8,1,384]{4,2,3,1,0:T(8,128)}, u32[]{:S(2)}, u32[]{:S(2)}) async-start(f32[32,1,8,1,384]{4,2,3,1,0:T(8,128)} %get-tuple-element.100), calls=%async_computation.11 | async-start | bytes 786432 | tf_op jit(solution)/shard_map/all_to_all | solution.py:190
  566.3 7.7 multiply_reduce_fusion
  582.1 7.7 multiply_reduce_fusion.1
  593.1 87.6 %all-reduce.7.cloned.1.call-done = (f32[128,1536]{1,0:T(8,128)}, f32[128,1536]{1,0:T(8,128)}, f32[128,1536]{1,0:T(8,128)}, f32[128,1536]{1,0:T(8,128)}) async-done(((f32[128,1536]{1,0:T(8,128)}, f32[128,1536]{1,0:T(8,128)}, f32[128,1536]{1,0:T(8,128)}, f32[128,1536]{1,0:T(8,128)}), (f32[128,1536]{1,0:T(8,128)}, f32[128,1536]{1,0:T(8,128)}, f32[128,1536]{1,0:T(8,128)}, ...) | async-done | bytes 3145744 | tf_op jit(solution)/shard_map/psum | solution.py:239
  689.2 4.1 fusion.33
  693.2 4.1 fusion.34
  697.3 3.4 fusion.168
  700.7 4.1 fusion.35
  704.8 3.3 fusion.166
  708.1 4.0 fusion.36
  712.1 76.1 %all-reduce.5.cloned.1.call-done = (f32[128,1536]{1,0:T(8,128)}, f32[128,1536]{1,0:T(8,128)}, f32[128,1536]{1,0:T(8,128)}, f32[128,1536]{1,0:T(8,128)}) async-done(((f32[128,1536]{1,0:T(8,128)}, f32[128,1536]{1,0:T(8,128)}, f32[128,1536]{1,0:T(8,128)}, f32[128,1536]{1,0:T(8,128)}), (f32[128,1536]{1,0:T(8,128)}, f32[128,1536]{1,0:T(8,128)}, f32[128,1536]{1,0:T(8,128)}, ...) | async-done | bytes 3145744 | tf_op jit(solution)/shard_map/psum | solution.py:245
  788.2 4.1 fusion.58
  (477 shorter events, 328.5 us)
Async XLA Ops:
  6.5 682.6 %copy-start = (bf16[1024,1536]{1,0:T(8,128)(2,1)S(1)}, bf16[1024,1536]{1,0:T(8,128)(2,1)}, u32[]{:S(2)}) copy-start(bf16[1024,1536]{1,0:T(8,128)(2,1)} %param.35) | copy-start | bytes 9437188
  9.8 19.8 %all-to-all-start = ((f32[32,1,1]{2,1,0:T(1,128)}), f32[32,1,1]{2,1,0:T(1,128)S(1)}, u32[]{:S(2)}, u32[]{:S(2)}) async-start(f32[32,1,1]{2,1,0:T(1,128)} %copy.719), calls=%async_computation | async-start | bytes 32768 | tf_op jit(solution)/shard_map/all_to_all | solution.py:153
  32.6 49.4 %all-to-all-start.9 = ((bf16[32,128,1,384]{3,1,2,0:T(8,128)(2,1)}), bf16[32,128,1,384]{3,1,2,0:T(8,128)(2,1)}, u32[]{:S(2)}, u32[]{:S(2)}) async-start(bf16[32,128,1,384]{3,1,2,0:T(8,128)(2,1)} %stack.22), calls=%async_computation.9 | async-start | bytes 6291456 | tf_op jit(solution)/shard_map/all_to_all | solution.py:136
  57.2 56.0 %copy-start.54 = (f32[512,6]{0,1:T(8,128)}, f32[512,6]{0,1:T(8,128)S(1)}, u32[]{:S(2)}) copy-start(f32[512,6]{0,1:T(8,128)S(1)} %fusion.110) | copy-start | bytes 36868
  57.4 50.3 %copy-start.81 = (s32[1024]{0:T(1024)}, s32[1024]{0:T(1024)S(1)}, u32[]{:S(2)}) copy-start(s32[1024]{0:T(1024)S(1)} %pad_clamp_fusion.2) | copy-start | bytes 12292
  63.8 18.2 %copy-start.36 = (bf16[128,384]{1,0:T(8,128)(2,1)S(1)}, bf16[128,384]{1,0:T(8,128)(2,1)}, u32[]{:S(2)}) copy-start(bf16[128,384]{1,0:T(8,128)(2,1)} %get-tuple-element.86) | copy-start | bytes 294916
  84.2 47.2 %all-to-all-start.5 = ((bf16[32,128,1,384]{3,1,2,0:T(8,128)(2,1)}), bf16[32,128,1,384]{3,1,2,0:T(8,128)(2,1)}, u32[]{:S(2)}, u32[]{:S(2)}) async-start(bf16[32,128,1,384]{3,1,2,0:T(8,128)(2,1)} %stack.20), calls=%async_computation.5 | async-start | bytes 6291456 | tf_op jit(solution)/shard_map/all_to_all | solution.py:136
  134.6 95.2 %all-to-all-start.13 = ((bf16[32,128,1,384]{3,1,2,0:T(8,128)(2,1)}), bf16[32,128,1,384]{3,1,2,0:T(8,128)(2,1)}, u32[]{:S(2)}, u32[]{:S(2)}) async-start(bf16[32,128,1,384]{3,1,2,0:T(8,128)(2,1)} %stack.24), calls=%async_computation.13 | async-start | bytes 6291456 | tf_op jit(solution)/shard_map/all_to_all | solution.py:136
  151.0 22.0 %copy-start.41 = (f32[32,8,1,6]{1,2,3,0:T(1,128)S(1)}, f32[32,8,1,6]{1,2,3,0:T(1,128)}, u32[]{:S(2)}) copy-start(f32[32,8,1,6]{1,2,3,0:T(1,128)} %get-tuple-element.76) | copy-start | bytes 18436
  168.8 19.6 %copy-start.73 = (f32[128,6]{0,1:T(8,128)S(1)}, f32[128,6]{0,1:T(8,128)}, u32[]{:S(2)}) copy-start(f32[128,6]{0,1:T(8,128)} %copy.819) | copy-start | bytes 9220
  169.8 20.0 %copy-start.58 = (f32[128,6]{0,1:T(8,128)S(1)}, f32[128,6]{0,1:T(8,128)}, u32[]{:S(2)}) copy-start(f32[128,6]{0,1:T(8,128)} %slice_add_fusion.1) | copy-start | bytes 9220
  204.0 14.3 %copy-start.35 = (bf16[2,128,384]{1,2,0:T(8,128)(2,1)S(1)}, bf16[2,128,384]{1,2,0:T(8,128)(2,1)}, u32[]{:S(2)}) copy-start(bf16[2,128,384]{1,2,0:T(8,128)(2,1)} %copy.786) | copy-start | bytes 589828
  213.2 16.4 %copy-start.84 = (s32[16]{0:T(128)S(1)}, s32[16]{0:T(128)}, u32[]{:S(2)}) copy-start(s32[16]{0:T(128)} %get-tuple-element.112) | copy-start | bytes 196
  232.9 49.4 %all-to-all-start.1 = ((bf16[32,128,1,384]{3,1,2,0:T(8,128)(2,1)}), bf16[32,128,1,384]{3,1,2,0:T(8,128)(2,1)}, u32[]{:S(2)}, u32[]{:S(2)}) async-start(bf16[32,128,1,384]{3,1,2,0:T(8,128)(2,1)} %stack.18), calls=%async_computation.1 | async-start | bytes 6291456 | tf_op jit(solution)/shard_map/all_to_all | solution.py:136
  242.6 111.3 %copy-start.61 = (s32[1024]{0:T(1024)}, s32[1024]{0:T(1024)S(1)}, u32[]{:S(2)}) copy-start(s32[1024]{0:T(1024)S(1)} %pad_clamp_fusion.3) | copy-start | bytes 12292
  242.7 84.9 %copy-start.86 = (pred[32]{0:T(512)(128)(4,1)}, pred[32]{0:T(512)(128)(4,1)S(1)}, u32[]{:S(2)}) copy-start(pred[32]{0:T(512)(128)(4,1)S(1)} %fusion.115) | copy-start | bytes 100
  330.6 30.8 %all-to-all-start.2 = ((f32[32,1,8,1,6]{2,3,4,1,0:T(1,128)}), f32[32,1,8,1,6]{2,3,4,1,0:T(1,128)}, u32[]{:S(2)}, u32[]{:S(2)}) async-start(f32[32,1,8,1,6]{2,3,4,1,0:T(1,128)} %copy.728), calls=%async_computation.2 | async-start | bytes 196608 | tf_op jit(solution)/shard_map/all_to_all | solution.py:164
  349.5 21.1 %copy-start.87 = (pred[32]{0:T(512)(128)(4,1)S(1)}, pred[32]{0:T(512)(128)(4,1)}, u32[]{:S(2)}) copy-start(pred[32]{0:T(512)(128)(4,1)} %copy-done.86) | copy-start | bytes 100
  355.3 19.6 %copy-start.51 = (f32[32,1,8,1,6]{0,2,4,3,1:T(8,128)S(1)}, f32[32,1,8,1,6]{0,2,4,3,1:T(8,128)}, u32[]{:S(2)}) copy-start(f32[32,1,8,1,6]{0,2,4,3,1:T(8,128)} %get-tuple-element.110) | copy-start | bytes 18436
  355.3 20.3 %copy-start.50 = (f32[32,1,8,1,6]{0,2,4,3,1:T(8,128)S(1)}, f32[32,1,8,1,6]{0,2,4,3,1:T(8,128)}, u32[]{:S(2)}) copy-start(f32[32,1,8,1,6]{0,2,4,3,1:T(8,128)} %get-tuple-element.107) | copy-start | bytes 18436
  355.3 21.0 %copy-start.49 = (f32[32,1,8,1,6]{0,2,4,3,1:T(8,128)S(1)}, f32[32,1,8,1,6]{0,2,4,3,1:T(8,128)}, u32[]{:S(2)}) copy-start(f32[32,1,8,1,6]{0,2,4,3,1:T(8,128)} %get-tuple-element.109) | copy-start | bytes 18436
  355.3 21.7 %copy-start.48 = (f32[32,1,8,1,6]{0,2,4,3,1:T(8,128)S(1)}, f32[32,1,8,1,6]{0,2,4,3,1:T(8,128)}, u32[]{:S(2)}) copy-start(f32[32,1,8,1,6]{0,2,4,3,1:T(8,128)} %get-tuple-element.104) | copy-start | bytes 18436
  357.2 30.8 %copy-start.46 = (f32[32,8,1,6]{0,1,3,2:T(8,128)S(1)}, f32[32,8,1,6]{0,1,3,2:T(8,128)}, u32[]{:S(2)}) copy-start(f32[32,8,1,6]{0,1,3,2:T(8,128)} %copy.730) | copy-start | bytes 18436
  357.2 30.8 %copy-start.47 = (f32[32,8,1,6]{0,1,3,2:T(8,128)S(1)}, f32[32,8,1,6]{0,1,3,2:T(8,128)}, u32[]{:S(2)}) copy-start(f32[32,8,1,6]{0,1,3,2:T(8,128)} %copy.751) | copy-start | bytes 18436
  358.4 56.3 %copy-start.44 = (f32[32,8,1,6]{0,1,3,2:T(8,128)S(1)}, f32[32,8,1,6]{0,1,3,2:T(8,128)}, u32[]{:S(2)}) copy-start(f32[32,8,1,6]{0,1,3,2:T(8,128)} %copy.777) | copy-start | bytes 18436
  358.4 56.3 %copy-start.45 = (f32[32,8,1,6]{0,1,3,2:T(8,128)S(1)}, f32[32,8,1,6]{0,1,3,2:T(8,128)}, u32[]{:S(2)}) copy-start(f32[32,8,1,6]{0,1,3,2:T(8,128)} %copy.809) | copy-start | bytes 18436
  360.0 14.1 %copy-start.52 = (f32[32,1,8,1,6]{0,2,4,3,1:T(8,128)S(1)}, f32[32,1,8,1,6]{0,2,4,3,1:T(8,128)}, u32[]{:S(2)}) copy-start(f32[32,1,8,1,6]{0,2,4,3,1:T(8,128)} %get-tuple-element.108) | copy-start | bytes 18436
  361.5 18.1 %all-to-all-start.6 = ((f32[32,1,8,1,6]{2,3,4,1,0:T(1,128)}), f32[32,1,8,1,6]{2,3,4,1,0:T(1,128)S(1)}, u32[]{:S(2)}, u32[]{:S(2)}) async-start(f32[32,1,8,1,6]{2,3,4,1,0:T(1,128)} %copy.749), calls=%async_computation.6 | async-start | bytes 196608 | tf_op jit(solution)/shard_map/all_to_all | solution.py:164
  379.6 17.3 %all-to-all-start.10 = ((f32[32,1,8,1,6]{2,3,4,1,0:T(1,128)}), f32[32,1,8,1,6]{2,3,4,1,0:T(1,128)S(1)}, u32[]{:S(2)}, u32[]{:S(2)}) async-start(f32[32,1,8,1,6]{2,3,4,1,0:T(1,128)} %copy.775), calls=%async_computation.10 | async-start | bytes 196608 | tf_op jit(solution)/shard_map/all_to_all | solution.py:164
  388.2 77.4 %copy-start.37 = (f32[64,8,6]{0,1,2:T(8,128)}, f32[64,8,6]{0,1,2:T(8,128)S(1)}, u32[]{:S(2)}) copy-start(f32[64,8,6]{0,1,2:T(8,128)S(1)} %get-tuple-element.124) | copy-start | bytes 36868
  396.9 13.2 %all-to-all-start.14 = ((f32[32,1,8,1,6]{2,3,4,1,0:T(1,128)}), f32[32,1,8,1,6]{2,3,4,1,0:T(1,128)S(1)}, u32[]{:S(2)}, u32[]{:S(2)}) async-start(f32[32,1,8,1,6]{2,3,4,1,0:T(1,128)} %copy.807), calls=%async_computation.14 | async-start | bytes 196608 | tf_op jit(solution)/shard_map/all_to_all | solution.py:164
  402.0 63.6 %copy-start.30 = (f32[16,8,6]{1,2,0:T(8,128)}, f32[16,8,6]{1,2,0:T(8,128)S(1)}, u32[]{:S(2)}) copy-start(f32[16,8,6]{1,2,0:T(8,128)S(1)} %select_reduce_fusion.3) | copy-start | bytes 9220
  410.1 12.8 %all-to-all-start.4 = ((f32[32,1,8,1,6]{2,3,4,1,0:T(1,128)}), f32[32,1,8,1,6]{2,3,4,1,0:T(1,128)S(1)}, u32[]{:S(2)}, u32[]{:S(2)}) async-start(f32[32,1,8,1,6]{2,3,4,1,0:T(1,128)} %copy.741), calls=%async_computation.4 | async-start | bytes 196608 | tf_op jit(solution)/shard_map/all_to_all | solution.py:177
  415.5 50.1 %copy-start.38 = (f32[64,8,6]{0,1,2:T(8,128)}, f32[64,8,6]{0,1,2:T(8,128)S(1)}, u32[]{:S(2)}) copy-start(f32[64,8,6]{0,1,2:T(8,128)S(1)} %get-tuple-element.125) | copy-start | bytes 36868
  415.5 50.1 %copy-start.39 = (f32[64,8,6]{0,1,2:T(8,128)}, f32[64,8,6]{0,1,2:T(8,128)S(1)}, u32[]{:S(2)}) copy-start(f32[64,8,6]{0,1,2:T(8,128)S(1)} %get-tuple-element.126) | copy-start | bytes 36868
  422.9 12.7 %all-to-all-start.16 = ((f32[32,1,8,1,6]{2,3,4,1,0:T(1,128)}), f32[32,1,8,1,6]{2,3,4,1,0:T(1,128)S(1)}, u32[]{:S(2)}, u32[]{:S(2)}) async-start(f32[32,1,8,1,6]{2,3,4,1,0:T(1,128)} %copy.830), calls=%async_computation.16 | async-start | bytes 196608 | tf_op jit(solution)/shard_map/all_to_all | solution.py:177
  435.6 13.5 %all-to-all-start.8 = ((f32[32,1,8,1,6]{2,3,4,1,0:T(1,128)}), f32[32,1,8,1,6]{2,3,4,1,0:T(1,128)}, u32[]{:S(2)}, u32[]{:S(2)}) async-start(f32[32,1,8,1,6]{2,3,4,1,0:T(1,128)} %copy.767), calls=%async_computation.8 | async-start | bytes 196608 | tf_op jit(solution)/shard_map/all_to_all | solution.py:177
  442.1 23.5 %copy-start.27 = (f32[16,8,6]{1,2,0:T(8,128)}, f32[16,8,6]{1,2,0:T(8,128)S(1)}, u32[]{:S(2)}) copy-start(f32[16,8,6]{1,2,0:T(8,128)S(1)} %get-tuple-element.10) | copy-start | bytes 9220
  442.1 23.6 %copy-start.28 = (f32[16,8,6]{1,2,0:T(8,128)}, f32[16,8,6]{1,2,0:T(8,128)S(1)}, u32[]{:S(2)}) copy-start(f32[16,8,6]{1,2,0:T(8,128)S(1)} %get-tuple-element.11) | copy-start | bytes 9220
  442.1 23.6 %copy-start.29 = (f32[16,8,6]{1,2,0:T(8,128)}, f32[16,8,6]{1,2,0:T(8,128)S(1)}, u32[]{:S(2)}) copy-start(f32[16,8,6]{1,2,0:T(8,128)S(1)} %get-tuple-element.12) | copy-start | bytes 9220
  449.1 16.5 %all-to-all-start.12 = ((f32[32,1,8,1,6]{2,3,4,1,0:T(1,128)}), f32[32,1,8,1,6]{2,3,4,1,0:T(1,128)}, u32[]{:S(2)}, u32[]{:S(2)}) async-start(f32[32,1,8,1,6]{2,3,4,1,0:T(1,128)} %copy.798), calls=%async_computation.12 | async-start | bytes 196608 | tf_op jit(solution)/shard_map/all_to_all | solution.py:177
  465.6 35.7 %all-to-all-start.3 = ((f32[32,1,8,1,384]{4,2,3,1,0:T(8,128)}), f32[32,1,8,1,384]{4,2,3,1,0:T(8,128)S(1)}, u32[]{:S(2)}, u32[]{:S(2)}) async-start(f32[32,1,8,1,384]{4,2,3,1,0:T(8,128)} %get-tuple-element.103), calls=%async_computation.3 | async-start | bytes 786432 | tf_op jit(solution)/shard_map/all_to_all | solution.py:190
  501.4 22.4 %all-to-all-start.7 = ((f32[32,1,8,1,384]{4,2,3,1,0:T(8,128)}), f32[32,1,8,1,384]{4,2,3,1,0:T(8,128)}, u32[]{:S(2)}, u32[]{:S(2)}) async-start(f32[32,1,8,1,384]{4,2,3,1,0:T(8,128)} %get-tuple-element.101), calls=%async_computation.7 | async-start | bytes 786432 | tf_op jit(solution)/shard_map/all_to_all | solution.py:190
  523.8 28.9 %all-to-all-start.15 = ((f32[32,1,8,1,384]{4,2,3,1,0:T(8,128)}), f32[32,1,8,1,384]{4,2,3,1,0:T(8,128)S(1)}, u32[]{:S(2)}, u32[]{:S(2)}) async-start(f32[32,1,8,1,384]{4,2,3,1,0:T(8,128)} %get-tuple-element.102), calls=%async_computation.15 | async-start | bytes 786432 | tf_op jit(solution)/shard_map/all_to_all | solution.py:190
  552.7 24.4 %all-to-all-start.11 = ((f32[32,1,8,1,384]{4,2,3,1,0:T(8,128)}), f32[32,1,8,1,384]{4,2,3,1,0:T(8,128)}, u32[]{:S(2)}, u32[]{:S(2)}) async-start(f32[32,1,8,1,384]{4,2,3,1,0:T(8,128)} %get-tuple-element.100), calls=%async_computation.11 | async-start | bytes 786432 | tf_op jit(solution)/shard_map/all_to_all | solution.py:190
  562.1 118.6 %all-reduce.7.cloned.1.call-start = ((), (), s32[]{:S(2)}) async-start(), calls=%async_computation.18 | async-start | bytes 6291456 | tf_op jit(solution)/shard_map/psum | solution.py:239
  593.0 90.7 %copy-start.80 = (f32[1536]{0:T(1024)S(1)}, f32[1536]{0:T(1024)}, u32[]{:S(2)}) copy-start(f32[1536]{0:T(1024)} %param.32) | copy-start | bytes 18436
  593.0 195.2 %all-reduce.5.cloned.1.call-start = ((), (), s32[]{:S(2)}) async-start(), calls=%async_computation.17 | async-start | bytes 6291456 | tf_op jit(solution)/shard_map/psum | solution.py:245
  (70 other events, 443.0 us)
Sparse Core Ops, SparseCore 0:
  593.1 87.4 all-reduce.6
  712.2 75.9 all-reduce.4
